TPU v7x, 512 devices: a whole 4x4x16 slice. The times are simulated.
512 devices in a mesh: tm: 32 (over z, core), row: 16 (over x, y).
Axes of the slice: x: 4, y: 4, z: 16, core: 2. Of those that a mesh axis runs over, the one named last changes fastest.
Arguments:
- video: bfloat16 [32, 4, 384, 1024], P('tm', None, 'row'), may hold values from -6 to 6
- stem_weight: bfloat16 [64, 4, 3, 3], replicated, may hold values from -1 to 1
- w_qkv: bfloat16 [1536, 2304], P('tm'), may hold values from -0.15625 to 0.15625
- decay: float32 [32, 6], P('tm'), may hold values from 0.04 to 1, as said below
Outputs:
- mixed: bfloat16 [32, 32, 128, 768], P('tm', 'row')
Inputs may be any that keep to these rules, and one draw needn't show every extreme that they name: decay lies in (0, 1].
All inputs are finite; a program needn't handle non-finite values.
Results may differ from a plain program's by a relative error of at most 0.012.
Values may be sent and summed in bfloat16 or wider, within the bound.
A program may use at most 128 MiB of HBM per device.

v0:
```python
import jax
import jax.numpy as jnp
from jax import lax
from jax.sharding import PartitionSpec as P

HEADS = 6


def shifted(block, axis, distance):
    devices = range(lax.axis_size(axis))
    route = [(i - distance, i) for i in devices if i - distance in devices]
    return lax.ppermute(block, axis, route)


def prefix_2(x, axis, join, neutral):
    place = lax.axis_index(axis)
    gathered = jax.tree.map(
        lambda a, kind: lax.all_gather(a.astype(kind), axis), x, (jnp.bfloat16, jnp.bfloat16)
    )
    state = jax.tree.map(lambda a, e: jnp.zeros_like(a) + jnp.asarray(e, a.dtype), x, neutral)

    def one(step, state):
        return join(
            state,
            jax.tree.map(
                lambda a, own: lax.dynamic_index_in_dim(a, step, 0, False).astype(own.dtype),
                gathered,
                x,
            ),
        )

    return lax.fori_loop(0, place, one, state)


def combine(first_pair, later_pair):
    return (first_pair[0] * later_pair[0], later_pair[0] * first_pair[1] + later_pair[1])


def summarize(frame_rates, outer_sums):
    factor = jnp.ones_like(frame_rates[0])
    summed = jnp.zeros_like(outer_sums[0])
    factor = factor * frame_rates[0]
    summed = frame_rates[0] * summed + outer_sums[0]
    return (factor, summed)


def unroll(prefix, frame_rates, outer_sums):
    running = prefix
    running = frame_rates[0] * running + outer_sums[0]
    collected = [running]
    return jnp.stack(collected, axis=0)


def local(video, stem_weight, w_qkv, decay):
    frames_dev = video.shape[0]
    upper_row = shifted(video[:, :, -1:, :], "row", 1)
    padded = jnp.concatenate([upper_row, video], axis=2)
    padded = jnp.pad(padded, ((0, 0), (0, 0), (0, 0), (1, 0)))
    stem_out = lax.conv_general_dilated(
        padded,
        stem_weight,
        (2, 2),
        "VALID",
        dimension_numbers=("NCHW", "OIHW", "NCHW"),
        preferred_element_type=jnp.float32,
    )
    features = jnp.tanh(stem_out).astype(jnp.bfloat16)
    channels = features.shape[1]
    patch_rows = features.shape[2] // 6
    patch_cols = features.shape[3] // 4
    frame_tokens = patch_rows * patch_cols
    shaped = features.reshape(frames_dev, channels, patch_rows, 6, patch_cols, 4).transpose(
        0, 2, 4, 1, 3, 5
    )
    tokens = shaped.reshape(frames_dev * frame_tokens, channels * 24)
    qkv_width = w_qkv.shape[1]
    empty = jnp.zeros((tokens.shape[0], qkv_width), jnp.float32)
    block_rows = lax.all_gather(w_qkv, "tm", axis=0, tiled=True)
    columns = lax.slice_in_dim(tokens, 0, block_rows.shape[0], axis=1)
    projected = (empty + jnp.dot(columns, block_rows, preferred_element_type=jnp.float32)).astype(
        jnp.bfloat16
    )
    inner_width = qkv_width // 3
    head_size = inner_width // HEADS
    queries = projected[:, :inner_width].reshape(frames_dev, frame_tokens, HEADS, head_size)
    keys = projected[:, inner_width : 2 * inner_width].reshape(
        frames_dev, frame_tokens, HEADS, head_size
    )
    values = projected[:, 2 * inner_width :].reshape(frames_dev, frame_tokens, HEADS, head_size)
    kv_local = jnp.einsum("fnhd,fnhe->fhde", keys, values, preferred_element_type=jnp.float32)
    head_rates = decay[:, :, None, None]
    kv_total = lax.psum(kv_local.astype(jnp.bfloat16), "row").astype(jnp.float32)
    factor, summed = summarize(head_rates, kv_total)
    prefix = prefix_2(
        (factor, summed), "tm", combine, (jnp.ones_like(factor), jnp.zeros_like(summed))
    )[1]
    states = unroll(prefix, head_rates, kv_total).astype(jnp.bfloat16)
    attended = jnp.einsum("fnhd,fhde->fnhe", queries, states, preferred_element_type=jnp.float32)
    attended = attended * lax.rsqrt(jnp.mean(attended * attended, axis=-1, keepdims=True) + 1e-06)
    return attended.reshape(frames_dev, patch_rows, patch_cols, inner_width).astype(jnp.bfloat16)


def solution(mesh):
    return jax.shard_map(
        local,
        mesh=mesh,
        in_specs=(P("tm", None, "row", None), P(), P("tm", None), P("tm", None)),
        out_specs=P("tm", "row", None, None),
        check_vma=False,
    )
```

profile of v0, /device:TPU:491, one launch (start us, length us, event | category | flops | bytes accessed | tf_op | source)
XLA Modules:
  0.0 324.3 jit_solution(5156422705934072437)
XLA Ops:
  8.2 3.2 collective-permute-start
  11.4 1.3 collective-permute-done
  13.8 1.3 reshape.102
  15.1 4.3 %copy.74 = bf16[4,25,1,8,130]{3,0,4,1,2:T(4,128)(2,1)S(1)} copy(bf16[4,25,1,8,130]{4,3,1,0,2:T(8,128)(2,1)} %reshape.102) | data formatting | bytes 416000 | tf_op jit(solution)/shard_map/conv_general_dilated | solution.py:59
  19.6 5.0 %fusion.3 = f32[12,8,65,64]{3,1,2,0:T(8,128)} fusion(bf16[64,4,3,3]{0,1,3,2:T(4,128)(2,1)S(1)} %copy-done, bf16[4,25,1,7,2]{3,0,4,1,2:T(4,128)(2,1)S(1)} %slice.18, bf16[4,25,1,8,130]{3,0,4,1,2:T(4,128)(2,1)S(1)} %copy.74), kind=kOutput, calls=%fused_computation.7 | convolution fusion | flops 29387520 | bytes 1812848 | tf_op jit(solution)/shard_map/conv_general_dilated | solution.py:59
  24.5 3.4 %copy.75 = f32[12,8,65,64]{2,3,1,0:T(8,128)S(1)} copy(f32[12,8,65,64]{3,1,2,0:T(8,128)} %fusion.3) | data formatting | bytes 3194880 | tf_op jit(solution)/shard_map/conv_general_dilated | solution.py:59
  28.4 1.2 copy.76
  29.6 1.2 reshape.91
  31.8 1.3 copy.78
  33.0 52.2 %all-gather.5.cloned.1.call-done = bf16[1536,2304]{1,0:T(8,128)(2,1)} async-done(((bf16[48,2304]{1,0:T(8,128)(2,1)}), bf16[1536,2304]{1,0:T(8,128)(2,1)}) %all-gather.5.cloned.1.call-update) | async-done | bytes 7077904 | tf_op jit(solution)/shard_map/all_gather | solution.py:78
  85.2 5.0 %convolution_convert_fusion = bf16[256,2304]{1,0:T(8,128)(2,1)S(1)} fusion(bf16[1536,2304]{1,0:T(8,128)(2,1)} %all-gather.5.cloned.1.call-done, bf16[192,8,2,128]{3,2,1,0:T(2,128)(2,1)S(1)} %bitcast.66), kind=kOutput, calls=%fused_computation.4 | convolution fusion | flops 1812529152 | bytes 9043968 | tf_op jit(solution)/shard_map/dot_general | solution.py:80
  91.7 108.5 %all-reduce.2.cloned.1.call-done = bf16[1,6,128,128]{3,2,1,0:T(8,128)(2,1)} async-done(((bf16[1,6,128,128]{3,2,1,0:T(8,128)(2,1)}), bf16[1,6,128,128]{3,2,1,0:T(8,128)(2,1)}) %all-reduce.2.cloned.1.call-update) | async-done | bytes 196624 | tf_op jit(solution)/shard_map/psum | solution.py:92
  200.3 1.7 fusion.9
  202.0 30.6 %all-gather.1 = bf16[32,1,6]{2,1,0:T(2,128)(2,1)S(1)} all-gather(bf16[1,1,6]{2,1,0:T(2,128)(2,1)S(1)} %convert_bitcast_fusion.1), channel_id=2, replica_groups=mesh['tm'=32,'row'=16] {'tm'}, dimensions={0}, use_global_device_ids=true | all-gather | bytes 396 | tf_op jit(solution)/shard_map/all_gather | solution.py:18
  233.0 48.6 %all-gather.7.cloned.1.call-done = bf16[32,6,128,128]{3,2,1,0:T(8,128)(2,1)} async-done(((bf16[1,6,128,128]{3,2,1,0:T(8,128)(2,1)}), bf16[32,6,128,128]{3,2,1,0:T(8,128)(2,1)}) %all-gather.7.cloned.1.call-update) | async-done | bytes 6291472 | tf_op jit(solution)/shard_map/all_gather | solution.py:18
  281.7 34.4 %while.12 = (s32[]{:T(128)}, f32[6,128,128]{2,1,0:T(8,128)S(1)}, s32[]{:T(128)}, bf16[32,6,1,1]{1,3,2,0:T(2,128)(2,1)S(1)}, bf16[32,6,128,128]{3,2,1,0:T(8,128)(2,1)}, /*index=5*/s32[]{:T(128)}, s32[]{:T(128)}, s32[]{:T(128)}) while((s32[]{:T(128)}, f32[6,128,128]{2,1,0:T(8,128)S(1)}, s32[]{:T(128)}, bf16[32,6,1,1]{1,3,2,0:T(2,128)(2,1)S(1)}, ...), condition=%wide.region_2.3_spmd, body=%wide.region_1.2_spmd.sunk | while | flops 294923 | bytes 983227 | solution.py:32
  281.7 1.1 convert_add_fusion.3
  284.0 1.1 convert_add_fusion.3
  285.1 1.1 convert_add_fusion.3
  288.4 1.1 convert_add_fusion.3
  291.7 1.1 convert_add_fusion.3
  295.1 1.1 convert_add_fusion.3
  298.4 1.1 convert_add_fusion.3
  301.7 1.1 convert_add_fusion.3
  (90 shorter events, 32.5 us)
Async XLA Ops:
  6.5 13.0 %copy-start = (bf16[64,4,3,3]{0,1,3,2:T(4,128)(2,1)S(1)}, bf16[64,4,3,3]{0,1,3,2:T(4,128)(2,1)}, u32[]{:S(2)}) copy-start(bf16[64,4,3,3]{0,1,3,2:T(4,128)(2,1)} %param.7) | copy-start | bytes 13828
  6.5 78.7 %all-gather.5.cloned.1.call-start = ((), (), s32[]{:S(2)}) async-start(), calls=%async_computation | async-start | bytes 7299072 | tf_op jit(solution)/shard_map/all_gather | solution.py:78
  7.3 193.0 %all-reduce.2.cloned.1.call-start = ((), (), s32[]{:S(2)}) async-start(), calls=%async_computation.1 | async-start | bytes 393216 | tf_op jit(solution)/shard_map/psum | solution.py:92
  8.2 4.5 %collective-permute-start = (bf16[1,4,1,1024]{3,2,1,0:T(2,128)(2,1)S(1)}, bf16[1,4,1,1024]{3,2,1,0:T(2,128)(2,1)S(1)}, u32[]{:S(2)}, u32[]{:S(2)}) collective-permute-start(bf16[1,4,1,1024]{3,2,1,0:T(2,128)(2,1)S(1)} %slice.12), channel_id=1, source_target_pairs={{0,1},{1,2},{2,3},{3,4},{4,5},{5,6},{6,7},{7,8},{8,9},{9,10},{10,1... | collective-permute-start | bytes 24584 | tf_op jit(solution)/shard_map/ppermute | solution.py:12
  24.5 3.4 %copy-start.2 = (pred[8,65]{1,0:T(8,128)(4,1)S(1)}, pred[8,65]{1,0:T(8,128)(4,1)}, u32[]{:S(2)}) copy-start(pred[8,65]{1,0:T(8,128)(4,1)} %constant.40) | copy-start | bytes 1564
  90.3 1.5 copy-start.3
  91.7 190.0 %all-gather.7.cloned.1.call-start = ((), (), s32[]{:S(2)}) async-start(), calls=%async_computation.2 | async-start | bytes 6488064 | tf_op jit(solution)/shard_map/all_gather | solution.py:18
  202.0 114.2 %copy-start.1 = (bf16[1,6,128,128]{3,2,1,0:T(8,128)(2,1)S(1)}, bf16[1,6,128,128]{3,2,1,0:T(8,128)(2,1)}, u32[]{:S(2)}) copy-start(bf16[1,6,128,128]{3,2,1,0:T(8,128)(2,1)} %all-reduce.2.cloned.1.call-done) | copy-start | bytes 589828
Sparse Core Ops, SparseCore 0:
  9.5 75.6 all-gather.4
  91.8 108.4 all-reduce.1
  202.4 79.2 all-gather.6
where the time goes:
time: 326 us; the launch traced here: 324 us
  waiting for transfers between devices  211 us (65%)
  other arithmetic  36.6 us (11%)
  blocking collectives  30.6 us (9%)
  local copies, waits for them, and re-layouts  16.7 us (5%)
  between operations  13.3 us (4%)
  matrix products  11.4 us (3%)
  starting transfers between devices  3.29 us (1%)
    psum x1, waiting for transfers between devices, local(): lax.psum(kv_local.astype(jnp.bfloat16), 'row').astype(jnp.float32)  109 us
    all_gather x1, waiting for transfers between devices, local(): block_rows = lax.all_gather(w_qkv, 'tm', axis=0, tiled=True)  52.2 us
    all_gather x1, waiting for transfers between devices, prefix_2(): lax.all_gather(a.astype(kind), axis)  48.6 us
    add x31, other arithmetic, combine(): later_pair[0] * first_pair[1] + later_pair[1]  33.1 us
    all_gather x1, blocking collectives, prefix_2(): lax.all_gather(a.astype(kind), axis)  30.6 us
    conv_general_dilated x4, local copies, waits for them, and re-layouts, local(): lax.conv_general_dilated(padded, stem_weight, (2, 2), 'VALID', dimension_...  9.06 us
  transfers between devices with their start and end apart: 4, of which 4 were waited for; matrix products, arithmetic and copies ran while one was open for 7% of the time, Pallas kernels for 0%

commit v1 on v0

--- a/solution.py
+++ b/solution.py
@@ -4,6 +4,12 @@
 from jax.sharding import PartitionSpec as P
 
 HEADS = 6
+
+
+def recast_rates(raw, bus_axis):
+    w1 = jax.lax.all_gather(raw, bus_axis)
+    q_next = jnp.sum(w1, 0)
+    return q_next
 
 
 def shifted(block, axis, distance):
@@ -89,7 +95,7 @@
     values = projected[:, 2 * inner_width :].reshape(frames_dev, frame_tokens, HEADS, head_size)
     kv_local = jnp.einsum("fnhd,fnhe->fhde", keys, values, preferred_element_type=jnp.float32)
     head_rates = decay[:, :, None, None]
-    kv_total = lax.psum(kv_local.astype(jnp.bfloat16), "row").astype(jnp.float32)
+    kv_total = recast_rates(kv_local.astype(jnp.bfloat16), "row").astype(jnp.float32)
     factor, summed = summarize(head_rates, kv_total)
     prefix = prefix_2(
         (factor, summed), "tm", combine, (jnp.ones_like(factor), jnp.zeros_like(summed))

time: 326 us -> 275 us (0.84)
  the two profiles are of different devices: /device:TPU:491 before, /device:TPU:485 now
where the time goes in v1:
time: 275 us; the launch traced here: 274 us
  waiting for transfers between devices  162 us (59%)
  other arithmetic  38.2 us (14%)
  blocking collectives  28.6 us (10%)
  local copies, waits for them, and re-layouts  16.6 us (6%)
  between operations  13.3 us (5%)
  matrix products  11.4 us (4%)
  starting transfers between devices  3.29 us (1%)
    all_gather x1, waiting for transfers between devices, recast_rates(): w1 = jax.lax.all_gather(raw, bus_axis)  59.8 us
    all_gather x1, waiting for transfers between devices, local(): block_rows = lax.all_gather(w_qkv, 'tm', axis=0, tiled=True)  50.2 us
    all_gather x1, waiting for transfers between devices, prefix_2(): lax.all_gather(a.astype(kind), axis)  47.6 us
    add x31, other arithmetic, combine(): later_pair[0] * first_pair[1] + later_pair[1]  33.1 us
    all_gather x1, blocking collectives, prefix_2(): lax.all_gather(a.astype(kind), axis)  28.6 us
    conv_general_dilated x4, local copies, waits for them, and re-layouts, local(): lax.conv_general_dilated(padded, stem_weight, (2, 2), 'VALID', dimension_...  9.01 us
  transfers between devices with their start and end apart: 4, of which 4 were waited for; matrix products, arithmetic and copies ran while one was open for 8% of the time, Pallas kernels for 0%

profile of v1, /device:TPU:485, one launch (start us, length us, event | category | flops | bytes accessed | tf_op | source)
XLA Modules:
  0.0 274.1 jit_solution(16727308106365300755)
XLA Ops:
  8.2 3.2 %collective-permute-start = (bf16[1,4,1,1024]{3,2,1,0:T(2,128)(2,1)S(1)}, bf16[1,4,1,1024]{3,2,1,0:T(2,128)(2,1)S(1)}, u32[]{:S(2)}, u32[]{:S(2)}) collective-permute-start(bf16[1,4,1,1024]{3,2,1,0:T(2,128)(2,1)S(1)} %slice.12), channel_id=1, source_target_pairs={{0,1},{1,2},{2,3},{3,4},{4,5},{5,6},{6,7},{7,8},{8,9},{9,10},{10,1... | collective-permute-start | bytes 24584 | tf_op jit(solution)/shard_map/ppermute | solution.py:18
  11.4 3.4 %collective-permute-done = bf16[1,4,1,1024]{3,2,1,0:T(2,128)(2,1)S(1)} collective-permute-done((bf16[1,4,1,1024]{3,2,1,0:T(2,128)(2,1)S(1)}, bf16[1,4,1,1024]{3,2,1,0:T(2,128)(2,1)S(1)}, u32[]{:S(2)}, u32[]{:S(2)}) %collective-permute-start) | collective-permute-done | bytes 8224 | tf_op jit(solution)/shard_map/ppermute | solution.py:18
  15.9 1.3 reshape.125
  17.2 4.3 %copy.74 = bf16[4,25,1,8,130]{3,0,4,1,2:T(4,128)(2,1)S(1)} copy(bf16[4,25,1,8,130]{4,3,1,0,2:T(8,128)(2,1)} %reshape.125) | data formatting | bytes 416000 | tf_op jit(solution)/shard_map/conv_general_dilated | solution.py:65
  21.6 5.0 %fusion.3 = f32[12,8,65,64]{3,1,2,0:T(8,128)} fusion(bf16[64,4,3,3]{0,1,3,2:T(4,128)(2,1)S(1)} %copy-done, bf16[4,25,1,7,2]{3,0,4,1,2:T(4,128)(2,1)S(1)} %slice.18, bf16[4,25,1,8,130]{3,0,4,1,2:T(4,128)(2,1)S(1)} %copy.74), kind=kOutput, calls=%fused_computation.7 | convolution fusion | flops 29387520 | bytes 1812848 | tf_op jit(solution)/shard_map/conv_general_dilated | solution.py:65
  26.6 3.3 %copy.75 = f32[12,8,65,64]{2,3,1,0:T(8,128)S(1)} copy(f32[12,8,65,64]{3,1,2,0:T(8,128)} %fusion.3) | data formatting | bytes 3194880 | tf_op jit(solution)/shard_map/conv_general_dilated | solution.py:65
  30.4 1.2 copy.76
  31.7 1.2 reshape.111
  33.8 1.3 copy.78
  35.1 50.2 %all-gather.7.cloned.1.call-done = bf16[1536,2304]{1,0:T(8,128)(2,1)} async-done(((bf16[48,2304]{1,0:T(8,128)(2,1)}), bf16[1536,2304]{1,0:T(8,128)(2,1)}) %all-gather.7.cloned.1.call-update) | async-done | bytes 7077904 | tf_op jit(solution)/shard_map/all_gather | solution.py:84
  85.3 5.0 %convolution_convert_fusion = bf16[256,2304]{1,0:T(8,128)(2,1)S(1)} fusion(bf16[1536,2304]{1,0:T(8,128)(2,1)} %all-gather.7.cloned.1.call-done, bf16[192,8,2,128]{3,2,1,0:T(2,128)(2,1)S(1)} %bitcast.62), kind=kOutput, calls=%fused_computation.4 | convolution fusion | flops 1812529152 | bytes 9043968 | tf_op jit(solution)/shard_map/dot_general | solution.py:86
  91.8 59.8 %all-gather.11.cloned.1.call-done = bf16[96,128,128]{2,1,0:T(8,128)(2,1)} async-done(((bf16[6,128,128]{2,1,0:T(8,128)(2,1)}), bf16[96,128,128]{2,1,0:T(8,128)(2,1)}) %all-gather.11.cloned.1.call-update) | async-done | bytes 3145744 | tf_op jit(solution)/shard_map/all_gather | solution.py:10
  151.6 2.5 reduce.3
  154.9 28.6 %all-gather.2 = bf16[32,1,6]{2,1,0:T(2,128)(2,1)S(1)} all-gather(bf16[1,1,6]{2,1,0:T(2,128)(2,1)S(1)} %convert_bitcast_fusion.1), channel_id=2, replica_groups=mesh['tm'=32,'row'=16] {'tm'}, dimensions={0}, use_global_device_ids=true | all-gather | bytes 396 | tf_op jit(solution)/shard_map/all_gather | solution.py:24
  183.9 47.6 %all-gather.9.cloned.1.call-done = bf16[32,6,128,128]{3,2,1,0:T(8,128)(2,1)} async-done(((bf16[1,6,128,128]{3,2,1,0:T(8,128)(2,1)}), bf16[32,6,128,128]{3,2,1,0:T(8,128)(2,1)}) %all-gather.9.cloned.1.call-update) | async-done | bytes 6291472 | tf_op jit(solution)/shard_map/all_gather | solution.py:24
  231.5 34.4 %while.12 = (s32[]{:T(128)}, f32[6,128,128]{2,1,0:T(8,128)S(1)}, s32[]{:T(128)}, bf16[32,6,1,1]{1,3,2,0:T(2,128)(2,1)S(1)}, bf16[32,6,128,128]{3,2,1,0:T(8,128)(2,1)}, /*index=5*/s32[]{:T(128)}, s32[]{:T(128)}, s32[]{:T(128)}) while((s32[]{:T(128)}, f32[6,128,128]{2,1,0:T(8,128)S(1)}, s32[]{:T(128)}, bf16[32,6,1,1]{1,3,2,0:T(2,128)(2,1)S(1)}, ...), condition=%wide.region_2.3_spmd, body=%wide.region_1.2_spmd.sunk | while | flops 294923 | bytes 983227 | solution.py:38
  233.8 1.1 convert_add_fusion.3
  237.1 1.1 convert_add_fusion.3
  240.4 1.1 convert_add_fusion.3
  243.8 1.1 convert_add_fusion.3
  244.9 1.1 convert_add_fusion.3
  247.1 1.1 convert_add_fusion.3
  248.2 1.1 convert_add_fusion.3
  251.5 1.1 convert_add_fusion.3
  (89 shorter events, 33.3 us)
Async XLA Ops:
  6.5 15.1 %copy-start = (bf16[64,4,3,3]{0,1,3,2:T(4,128)(2,1)S(1)}, bf16[64,4,3,3]{0,1,3,2:T(4,128)(2,1)}, u32[]{:S(2)}) copy-start(bf16[64,4,3,3]{0,1,3,2:T(4,128)(2,1)} %param.7) | copy-start | bytes 13828
  6.5 78.7 %all-gather.7.cloned.1.call-start = ((), (), s32[]{:S(2)}) async-start(), calls=%async_computation | async-start | bytes 7299072 | tf_op jit(solution)/shard_map/all_gather | solution.py:84
  7.3 144.3 %all-gather.11.cloned.1.call-start = ((), (), s32[]{:S(2)}) async-start(), calls=%async_computation.2 | async-start | bytes 3342336 | tf_op jit(solution)/shard_map/all_gather | solution.py:10
  8.2 6.6 %collective-permute-start = (bf16[1,4,1,1024]{3,2,1,0:T(2,128)(2,1)S(1)}, bf16[1,4,1,1024]{3,2,1,0:T(2,128)(2,1)S(1)}, u32[]{:S(2)}, u32[]{:S(2)}) collective-permute-start(bf16[1,4,1,1024]{3,2,1,0:T(2,128)(2,1)S(1)} %slice.12), channel_id=1, source_target_pairs={{0,1},{1,2},{2,3},{3,4},{4,5},{5,6},{6,7},{7,8},{8,9},{9,10},{10,1... | collective-permute-start | bytes 24584 | tf_op jit(solution)/shard_map/ppermute | solution.py:18
  26.6 3.3 %copy-start.1 = (pred[8,65]{1,0:T(8,128)(4,1)S(1)}, pred[8,65]{1,0:T(8,128)(4,1)}, u32[]{:S(2)}) copy-start(pred[8,65]{1,0:T(8,128)(4,1)} %constant.42) | copy-start | bytes 1564
  90.3 1.5 copy-start.2
  91.7 139.7 %all-gather.9.cloned.1.call-start = ((), (), s32[]{:S(2)}) async-start(), calls=%async_computation.1 | async-start | bytes 6488064 | tf_op jit(solution)/shard_map/all_gather | solution.py:24
Sparse Core Ops, SparseCore 0:
  9.5 75.7 all-gather.6
  91.9 59.6 all-gather.10
  155.0 76.4 all-gather.8

commit v2 on v0

--- a/solution.py
+++ b/solution.py
@@ -75,7 +75,9 @@
     tokens = shaped.reshape(frames_dev * frame_tokens, channels * 24)
     qkv_width = w_qkv.shape[1]
     empty = jnp.zeros((tokens.shape[0], qkv_width), jnp.float32)
-    block_rows = lax.all_gather(w_qkv, "tm", axis=0, tiled=True)
+    block_rows = jnp.concatenate(
+        lax.all_to_all(jnp.stack([w_qkv] * lax.axis_size("tm"), 0), "tm", 0, 0), 0
+    )
     columns = lax.slice_in_dim(tokens, 0, block_rows.shape[0], axis=1)
     projected = (empty + jnp.dot(columns, block_rows, preferred_element_type=jnp.float32)).astype(
         jnp.bfloat16

time: 326 us -> 570 us (1.75)
  the two profiles are of different devices: /device:TPU:491 before, /device:TPU:485 now
where the time goes in v2:
time: 570 us; the launch traced here: 569 us
  waiting for transfers between devices  444 us (78%)
  other arithmetic  35.7 us (6%)
  blocking collectives  30.8 us (5%)
  local copies, waits for them, and re-layouts  20.1 us (4%)
  between operations  13.6 us (2%)
  starting transfers between devices  12.9 us (2%)
  matrix products  11.3 us (2%)
    all_to_all x1, waiting for transfers between devices, local(): lax.all_to_all(jnp.stack([w_qkv] * lax.axis_size('tm'), 0), 'tm', 0, 0)  274 us
    psum x1, waiting for transfers between devices, local(): lax.psum(kv_local.astype(jnp.bfloat16), 'row').astype(jnp.float32)  119 us
    all_gather x1, waiting for transfers between devices, prefix_2(): lax.all_gather(a.astype(kind), axis)  48 us
    add x31, other arithmetic, combine(): later_pair[0] * first_pair[1] + later_pair[1]  33.1 us
    all_gather x1, blocking collectives, prefix_2(): lax.all_gather(a.astype(kind), axis)  30.8 us
  transfers between devices with their start and end apart: 4, of which 4 were waited for; matrix products, arithmetic and copies ran while one was open for 3% of the time, Pallas kernels for 0%

profile of v2, /device:TPU:485, one launch (start us, length us, event | category | flops | bytes accessed | tf_op | source)
XLA Modules:
  0.0 569.2 jit_solution(3549427136015320391)
XLA Ops:
  6.5 4.3 stack.2
  10.9 9.6 %all-to-all-start = ((bf16[32,48,2304]{2,1,0:T(8,128)(2,1)}), bf16[32,48,2304]{2,1,0:T(8,128)(2,1)}, u32[]{:S(2)}, u32[]{:S(2)}) async-start(bf16[32,48,2304]{2,1,0:T(8,128)(2,1)} %stack.2), calls=%async_computation | async-start | bytes 14155776 | tf_op jit(solution)/shard_map/all_to_all | solution.py:79
  20.5 3.2 collective-permute-start
  23.7 3.4 collective-permute-done
  27.3 1.3 reshape.108
  28.7 4.3 copy.74
  33.1 4.9 fusion.3
  38.0 3.3 copy.75
  41.7 1.2 copy.76
  43.0 1.2 reshape.97
  45.1 1.3 copy.78
  46.4 273.6 %all-to-all-done = bf16[32,48,2304]{2,1,0:T(8,128)(2,1)} async-done(((bf16[32,48,2304]{2,1,0:T(8,128)(2,1)}), bf16[32,48,2304]{2,1,0:T(8,128)(2,1)}, u32[]{:S(2)}, u32[]{:S(2)}) %all-to-all-start) | async-done | bytes 7077920 | tf_op jit(solution)/shard_map/all_to_all | solution.py:79
  319.9 5.0 convolution_convert_fusion
  326.5 118.9 %all-reduce.2.cloned.1.call-done = bf16[1,6,128,128]{3,2,1,0:T(8,128)(2,1)} async-done(((bf16[1,6,128,128]{3,2,1,0:T(8,128)(2,1)}), bf16[1,6,128,128]{3,2,1,0:T(8,128)(2,1)}) %all-reduce.2.cloned.1.call-update) | async-done | bytes 196624 | tf_op jit(solution)/shard_map/psum | solution.py:94
  445.4 1.7 fusion.9
  447.2 30.8 %all-gather.1 = bf16[32,1,6]{2,1,0:T(2,128)(2,1)S(1)} all-gather(bf16[1,1,6]{2,1,0:T(2,128)(2,1)S(1)} %convert_bitcast_fusion.1), channel_id=2, replica_groups=mesh['tm'=32,'row'=16] {'tm'}, dimensions={0}, use_global_device_ids=true | all-gather | bytes 396 | tf_op jit(solution)/shard_map/all_gather | solution.py:18
  478.3 48.0 %all-gather.4.cloned.1.call-done = bf16[32,6,128,128]{3,2,1,0:T(8,128)(2,1)} async-done(((bf16[1,6,128,128]{3,2,1,0:T(8,128)(2,1)}), bf16[32,6,128,128]{3,2,1,0:T(8,128)(2,1)}) %all-gather.4.cloned.1.call-update) | async-done | bytes 6291472 | tf_op jit(solution)/shard_map/all_gather | solution.py:18
  526.4 34.3 %while.12 = (s32[]{:T(128)}, f32[6,128,128]{2,1,0:T(8,128)S(1)}, s32[]{:T(128)}, bf16[32,6,1,1]{1,3,2,0:T(2,128)(2,1)S(1)}, bf16[32,6,128,128]{3,2,1,0:T(8,128)(2,1)}, /*index=5*/s32[]{:T(128)}, s32[]{:T(128)}, s32[]{:T(128)}) while((s32[]{:T(128)}, f32[6,128,128]{2,1,0:T(8,128)S(1)}, s32[]{:T(128)}, bf16[32,6,1,1]{1,3,2,0:T(2,128)(2,1)S(1)}, ...), condition=%wide.region_2.3_spmd, body=%wide.region_1.2_spmd.sunk | while | flops 294923 | bytes 983235 | solution.py:32
  529.7 1.1 convert_add_fusion.3
  530.8 1.1 convert_add_fusion.3
  531.9 1.1 convert_add_fusion.3
  536.4 1.1 convert_add_fusion.3
  537.5 1.1 convert_add_fusion.3
  538.6 1.1 convert_add_fusion.3
  (92 shorter events, 32.2 us)
Async XLA Ops:
  6.5 26.5 %copy-start = (bf16[64,4,3,3]{0,1,3,2:T(4,128)(2,1)S(1)}, bf16[64,4,3,3]{0,1,3,2:T(4,128)(2,1)}, u32[]{:S(2)}) copy-start(bf16[64,4,3,3]{0,1,3,2:T(4,128)(2,1)} %param.7) | copy-start | bytes 13828
  10.9 9.6 %copy-start.2 = (bf16[1,4,24,1024]{3,2,1,0:T(8,128)(2,1)S(1)}, bf16[1,4,24,1024]{3,2,1,0:T(8,128)(2,1)}, u32[]{:S(2)}) copy-start(bf16[1,4,24,1024]{3,2,1,0:T(8,128)(2,1)} %param.6) | copy-start | bytes 589828
  10.9 309.1 %all-to-all-start = ((bf16[32,48,2304]{2,1,0:T(8,128)(2,1)}), bf16[32,48,2304]{2,1,0:T(8,128)(2,1)}, u32[]{:S(2)}, u32[]{:S(2)}) async-start(bf16[32,48,2304]{2,1,0:T(8,128)(2,1)} %stack.2), calls=%async_computation | async-start | bytes 14155776 | tf_op jit(solution)/shard_map/all_to_all | solution.py:79
  20.4 425.0 %all-reduce.2.cloned.1.call-start = ((), (), s32[]{:S(2)}) async-start(), calls=%async_computation.1 | async-start | bytes 393216 | tf_op jit(solution)/shard_map/psum | solution.py:94
  20.5 6.6 %collective-permute-start = (bf16[1,4,1,1024]{3,2,1,0:T(2,128)(2,1)S(1)}, bf16[1,4,1,1024]{3,2,1,0:T(2,128)(2,1)S(1)}, u32[]{:S(2)}, u32[]{:S(2)}) collective-permute-start(bf16[1,4,1,1024]{3,2,1,0:T(2,128)(2,1)S(1)} %slice.12), channel_id=1, source_target_pairs={{0,1},{1,2},{2,3},{3,4},{4,5},{5,6},{6,7},{7,8},{8,9},{9,10},{10,1... | collective-permute-start | bytes 24584 | tf_op jit(solution)/shard_map/ppermute | solution.py:12
  38.0 3.3 copy-start.3
  325.0 1.5 copy-start.4
  326.4 199.9 %all-gather.4.cloned.1.call-start = ((), (), s32[]{:S(2)}) async-start(), calls=%async_computation.2 | async-start | bytes 6488064 | tf_op jit(solution)/shard_map/all_gather | solution.py:18
  447.1 113.5 %copy-start.1 = (bf16[1,6,128,128]{3,2,1,0:T(8,128)(2,1)S(1)}, bf16[1,6,128,128]{3,2,1,0:T(8,128)(2,1)}, u32[]{:S(2)}) copy-start(bf16[1,6,128,128]{3,2,1,0:T(8,128)(2,1)} %all-reduce.2.cloned.1.call-done) | copy-start | bytes 589828
Sparse Core Ops, SparseCore 0:
  326.5 118.8 all-reduce.1
  447.5 78.7 all-gather.3
